TPU v7x, 128 devices: a whole 4x4x4 slice. The times are simulated.
128 devices in a mesh: dp: 4 (over z), fsdp: 32 (over x, y, core).
Axes of the slice: x: 4, y: 4, z: 4, core: 2. Of those that a mesh axis runs over, the one named last changes fastest.
Arguments:
- tokens: bfloat16 [32768, 6144], P(('dp', 'fsdp')), may hold values from -6 to 6
- cotangent: bfloat16 [32768, 6144], P(('dp', 'fsdp')), may hold values from -6 to 6
- up_weight_blocks: bfloat16 [128, 128, 128], P('fsdp'), may hold values from -0.5 to 0.5
- down_weight_blocks: bfloat16 [128, 128, 128], P('fsdp'), may hold values from -0.5 to 0.5
- block_rows: int32 [128], replicated, may hold values from 0 to 47, as said below
- block_cols: int32 [128], replicated, may hold values from 0 to 191
- owner_counts: int32 [32], replicated, may hold values from 1 to 4, as said below
Outputs:
- output: bfloat16 [32768, 6144], P(('dp', 'fsdp'))
- input_grad: bfloat16 [32768, 6144], P(('dp', 'fsdp'))
- up_grad: float32 [128, 128, 128], P('fsdp')
- down_grad: float32 [128, 128, 128], P('fsdp')
Inputs may be any that keep to these rules, and one draw needn't show every extreme that they name: Owner o has owner_counts[o] live slots, its first ones; some owner has all 4 live. All 128 slots name distinct (block_rows, block_cols) pairs.
All inputs are finite; a program needn't handle non-finite values.
Results may differ from a plain program's by a relative error of at most 0.0049.
Values may be sent and summed in bfloat16 or wider, within the bound.
A program may use at most 256 MiB of HBM per device.

v0:
```python
import math
import jax
import jax.numpy as jnp
from jax import lax
from jax.sharding import PartitionSpec as P

D = 6144
FF = 24576
BLOCK_EDGE = 128
SLOTS = 4
gelu_scale = 0.7978845608028654
cubic_coef = 0.044715


def gelu_parts(values):
    inner_arg = gelu_scale * (values + cubic_coef * values * values * values)
    tanh_val = jnp.tanh(inner_arg)
    gelu_value = 0.5 * values * (1.0 + tanh_val)
    gelu_slope = 0.5 * (1.0 + tanh_val) + 0.5 * values * (
        1.0 - tanh_val * tanh_val
    ) * gelu_scale * (1.0 + 3.0 * cubic_coef * values * values)
    return (gelu_value, gelu_slope)


def to_blocks(source):
    token_count = source.shape[0]
    return source.reshape(token_count, source.shape[1] // BLOCK_EDGE, BLOCK_EDGE).transpose(1, 0, 2)


def from_blocks(blocks):
    return blocks.transpose(1, 0, 2).reshape(blocks.shape[1], blocks.shape[0] * BLOCK_EDGE)


def one_hot_table(index_list, width, dtype):
    return (index_list[:, None] == jnp.arange(width, dtype=jnp.int32)[None, :]).astype(dtype)


def pick_blocks(blocks, index_list):
    table = one_hot_table(index_list, blocks.shape[0], jnp.bfloat16)
    return jnp.einsum("sr,rnk->snk", table, blocks, preferred_element_type=jnp.float32).astype(
        jnp.bfloat16
    )


def spread_blocks(contrib, index_list, width):
    table = one_hot_table(index_list, width, jnp.float32)
    return jnp.einsum(
        "sc,snj->cnj",
        table,
        contrib,
        preferred_element_type=jnp.float32,
        precision=lax.Precision.HIGHEST,
    )


def on_device(
    tokens, cotangent, up_weight_blocks, down_weight_blocks, block_rows, block_cols, owner_counts
):
    token_count = tokens.shape[0]
    total_slots = block_rows.shape[0]
    row_blocks = D // BLOCK_EDGE
    col_blocks = FF // BLOCK_EDGE
    slot_position = jnp.arange(total_slots, dtype=jnp.int32)
    live_mask = slot_position % SLOTS < owner_counts[slot_position // SLOTS]
    x_blocks = to_blocks(tokens)
    dy_blocks = to_blocks(cotangent)

    def slot_info():
        return (block_rows, block_cols, live_mask.astype(jnp.bfloat16)[:, None, None])

    up_whole = lax.all_gather(up_weight_blocks, "fsdp", axis=0, tiled=True)
    row_ids, col_ids, keep_mask = slot_info()
    picked = pick_blocks(x_blocks, row_ids)
    contrib = jnp.einsum(
        "snk,skj->snj", picked, up_whole * keep_mask, preferred_element_type=jnp.float32
    )
    pre_act = spread_blocks(contrib, col_ids, col_blocks)
    gelu_value, gelu_slope = gelu_parts(pre_act)
    hidden = gelu_value.astype(jnp.bfloat16)
    row_ids, col_ids, keep_mask = slot_info()
    weights = lax.all_gather(down_weight_blocks, "fsdp", axis=0, tiled=True) * keep_mask
    h_pick = pick_blocks(hidden, col_ids)
    dy_pick = pick_blocks(dy_blocks, row_ids)
    out_part = jnp.einsum("snk,skj->snj", h_pick, weights, preferred_element_type=jnp.float32)
    back_part = jnp.einsum("snj,skj->snk", dy_pick, weights, preferred_element_type=jnp.float32)
    out_sum = spread_blocks(out_part, row_ids, row_blocks)
    hidden_grad = spread_blocks(back_part, col_ids, col_blocks)
    output = from_blocks(out_sum.astype(jnp.bfloat16))
    pre_grad = (hidden_grad * gelu_slope).astype(jnp.bfloat16)
    row_ids, col_ids, keep_mask = slot_info()
    picked = pick_blocks(pre_grad, col_ids)
    contrib = jnp.einsum(
        "snj,skj->snk", picked, up_whole * keep_mask, preferred_element_type=jnp.float32
    )
    in_sum = spread_blocks(contrib, row_ids, row_blocks)
    input_grad = from_blocks(in_sum.astype(jnp.bfloat16))
    dp_groups = lax.axis_size("dp")
    fsdp_owners = lax.axis_size("fsdp")
    grad_scale = 1.0 / math.sqrt(token_count * dp_groups * fsdp_owners)
    slot_list = jnp.arange(lax.axis_size("fsdp") * SLOTS, dtype=jnp.int32)
    keep_mask = live_mask[slot_list].astype(jnp.float32)[:, None, None]
    x_pick = pick_blocks(x_blocks, block_rows[slot_list])
    p_pick = pick_blocks(pre_grad, block_cols[slot_list])
    up_local = lax.psum_scatter(
        jnp.einsum("snk,snj->skj", x_pick, p_pick, preferred_element_type=jnp.float32) * keep_mask,
        "fsdp",
        scatter_dimension=0,
        tiled=True,
    )
    slot_list = jnp.arange(lax.axis_size("fsdp") * SLOTS, dtype=jnp.int32)
    keep_mask = live_mask[slot_list].astype(jnp.float32)[:, None, None]
    h_pick = pick_blocks(hidden, block_cols[slot_list])
    dy_pick = pick_blocks(dy_blocks, block_rows[slot_list])
    down_local = lax.psum_scatter(
        jnp.einsum("snk,snj->skj", h_pick, dy_pick, preferred_element_type=jnp.float32) * keep_mask,
        "fsdp",
        scatter_dimension=0,
        tiled=True,
    )
    up_grad, down_grad = lax.psum((up_local, down_local), "dp")
    return (output, input_grad, up_grad * grad_scale, down_grad * grad_scale)


def solution(mesh):
    in_specs = (
        P(("dp", "fsdp"), None),
        P(("dp", "fsdp"), None),
        P("fsdp", None, None),
        P("fsdp", None, None),
        P(),
        P(),
        P(),
    )
    out_specs = (
        P(("dp", "fsdp"), None),
        P(("dp", "fsdp"), None),
        P("fsdp", None, None),
        P("fsdp", None, None),
    )
    return jax.shard_map(
        on_device, mesh=mesh, in_specs=in_specs, out_specs=out_specs, check_vma=False
    )
```

profile of v0, /device:TPU:0, one launch (start us, length us, event | category | flops | bytes accessed | tf_op | source)
XLA Modules:
  0.0 445.9 jit_solution(9239581407377566130)
XLA Ops:
  7.2 0.7 all-gather.3.cloned.1.call-update
  8.0 0.7 all-gather.5.cloned.1.call-update
  8.7 4.4 copy.23
  13.2 0.7 copy.25
  13.9 1.2 gather_fusion.2
  15.2 1.2 gather_fusion.1
  16.5 1.2 gather_fusion
  17.7 1.4 gather_fusion.3
  19.1 7.5 %convolution_convert_fusion.7 = bf16[128,256,128]{2,0,1:T(8,128)(2,1)} fusion(bf16[256,48,128]{2,1,0:T(8,128)(2,1)} %bitcast.50, s32[128]{0:T(128)S(1)} %copy-done.2), kind=kOutput, calls=%fused_computation.43 | convolution fusion | flops 406853632 | bytes 11534848 | tf_op jit(solution)/shard_map/sr,rnk->snk/dot_general | solution.py:40
  26.6 5.6 %convolution_convert_fusion.5 = bf16[128,256,128]{2,0,1:T(8,128)(2,1)} fusion(bf16[256,48,128]{2,1,0:T(8,128)(2,1)S(1)} %bitcast.48, s32[128]{0:T(128)S(1)} %copy-done.2), kind=kOutput, calls=%fused_computation.41 | convolution fusion | flops 406853632 | bytes 11534848 | tf_op jit(solution)/shard_map/sr,rnk->snk/dot_general | solution.py:40
  32.2 5.6 %convolution_convert_fusion.3 = bf16[128,256,128]{2,0,1:T(8,128)(2,1)} fusion(bf16[256,48,128]{2,1,0:T(8,128)(2,1)S(1)} %bitcast.51, s32[128]{0:T(128)S(1)} %gather_fusion.1), kind=kOutput, calls=%fused_computation.39 | convolution fusion | flops 406853632 | bytes 11534848 | tf_op jit(solution)/shard_map/sr,rnk->snk/dot_general | solution.py:40
  37.9 20.9 %all-gather.3.cloned.1.call-done = bf16[128,128,128]{2,1,0:T(8,128)(2,1)} async-done(((bf16[4,128,128]{2,1,0:T(8,128)(2,1)}), bf16[128,128,128]{2,1,0:T(8,128)(2,1)}) %all-gather.3.cloned.1.call-update) | async-done | bytes 4194320 | tf_op jit(solution)/shard_map/all_gather | solution.py:71
  58.7 18.8 %fusion.27 = f32[128,256,128]{2,1,0:T(8,128)} fusion(bf16[128,256,128]{2,0,1:T(8,128)(2,1)} %convolution_convert_fusion.7, bf16[128,128,128]{2,1,0:T(8,128)(2,1)} %all-gather.3.cloned.1.call-done, bf16[128]{0:T(256)(128)(2,1)S(1)} %get-tuple-element.6), kind=kOutput, calls=%fused_computation.34 | convolution fusion | flops 1075838976 | bytes 29360384 | tf_op jit(solution)/shard_map/snk,skj->snj/dot_general | solution.py:74
  77.6 30.3 %fusion.13 = f32[192,256,128]{2,0,1:T(8,128)} fusion(f32[128,256,128]{2,1,0:T(8,128)} %fusion.27, s32[128]{0:T(128)S(1)} %copy-done.4), kind=kOutput, calls=%fused_computation.20 | convolution fusion | flops 9663700992 | bytes 41943552 | tf_op jit(solution)/shard_map/sc,snj->cnj/dot_general | solution.py:47
  107.9 18.5 %fusion.23 = f32[128,256,128]{2,1,0:T(8,128)} fusion(bf16[128,256,128]{2,0,1:T(8,128)(2,1)} %convolution_convert_fusion.5, bf16[128,128,128]{2,1,0:T(8,128)(2,1)} %all-gather.5.cloned.1.call-done, bf16[128]{0:T(256)(128)(2,1)S(1)} %get-tuple-element.6), kind=kOutput, calls=%fused_computation.30 | convolution fusion | flops 1075838976 | bytes 29360384 | tf_op jit(solution)/shard_map/snj,skj->snk/dot_general | solution.py:85
  126.5 44.2 %fusion.6 = bf16[192,256,128]{2,0,1:T(8,128)(2,1)S(1)} fusion(f32[192,256,128]{2,0,1:T(8,128)} %fusion.13, f32[128,256,128]{2,1,0:T(8,128)} %fusion.23, s32[128]{0:T(128)S(1)} %copy-done.4), kind=kOutput, calls=%fused_computation.12 | convolution fusion | flops 9783238656 | bytes 54526464 | tf_op jit(solution)/shard_map/sc,snj->cnj/dot_general | solution.py:47
  170.7 4.6 %copy-done.5 = bf16[192,256,128]{2,0,1:T(8,128)(2,1)} copy-done((bf16[192,256,128]{2,0,1:T(8,128)(2,1)}, bf16[192,256,128]{2,0,1:T(8,128)(2,1)S(1)}, u32[]{:S(2)}) %copy-start.5) | copy-done | bytes 12582936
  175.3 5.6 %convolution_convert_fusion.2 = bf16[128,256,128]{2,0,1:T(8,128)(2,1)} fusion(bf16[192,256,128]{2,0,1:T(8,128)(2,1)S(1)} %fusion.6, s32[128]{0:T(128)S(1)} %gather_fusion.2), kind=kOutput, calls=%fused_computation.38 | convolution fusion | flops 1614831616 | bytes 20972032 | tf_op jit(solution)/shard_map/sr,rnk->snk/dot_general | solution.py:40
  180.9 23.2 %broadcast_multiply_fusion.1 = f32[128,128,128]{2,1,0:T(8,128)} fusion(f32[128]{0:T(128)S(1)} %convert_element_type.86, bf16[128,256,128]{2,0,1:T(8,128)(2,1)} %convolution_convert_fusion.2, bf16[128,256,128]{2,0,1:T(8,128)(2,1)} %convolution_convert_fusion.3), kind=kOutput, calls=%fused_computation.45 | convolution fusion | flops 1075838976 | bytes 25166336 | tf_op jit(solution)/shard_map/snk,snj->skj/dot_general | solution.py:105
  204.2 5.6 %convolution_convert_fusion = bf16[128,256,128]{2,0,1:T(8,128)(2,1)} fusion(bf16[256,48,128]{2,1,0:T(8,128)(2,1)S(1)} %bitcast.49, s32[128]{0:T(128)S(1)} %gather_fusion.1), kind=kOutput, calls=%fused_computation.36 | convolution fusion | flops 406853632 | bytes 11534848 | tf_op jit(solution)/shard_map/sr,rnk->snk/dot_general | solution.py:40
  209.8 17.1 %convolution_convert_fusion.1 = bf16[128,256,128]{2,0,1:T(8,128)(2,1)} fusion(s32[128]{0:T(128)S(1)} %gather_fusion.2, f32[192,256,128]{2,0,1:T(8,128)} %fusion.13), kind=kOutput, calls=%fused_computation.37 | convolution fusion | flops 1671454720 | bytes 33554944 | tf_op jit(solution)/shard_map/sr,rnk->snk/dot_general | solution.py:40
  226.9 23.8 %broadcast_multiply_fusion = f32[128,128,128]{2,1,0:T(8,128)} fusion(f32[128]{0:T(128)S(1)} %convert_element_type.86, bf16[128,256,128]{2,0,1:T(8,128)(2,1)} %convolution_convert_fusion, bf16[128,256,128]{2,0,1:T(8,128)(2,1)} %convolution_convert_fusion.1), kind=kOutput, calls=%fused_computation.44 | convolution fusion | flops 1075838976 | bytes 25166336 | tf_op jit(solution)/shard_map/snk,snj->skj/dot_general | solution.py:115
  250.8 11.0 %convolution_convert_fusion.4 = bf16[128,256,128]{2,0,1:T(8,128)(2,1)} fusion(bf16[192,256,128]{2,0,1:T(8,128)(2,1)} %copy-done.5, s32[128]{0:T(128)S(1)} %copy-done.4), kind=kOutput, calls=%fused_computation.40 | convolution fusion | flops 1614831616 | bytes 20972032 | tf_op jit(solution)/shard_map/sr,rnk->snk/dot_general | solution.py:40
  261.8 18.8 %fusion.21 = f32[128,256,128]{2,1,0:T(8,128)} fusion(bf16[128,256,128]{2,0,1:T(8,128)(2,1)} %convolution_convert_fusion.4, bf16[128,128,128]{2,1,0:T(8,128)(2,1)} %all-gather.3.cloned.1.call-done, bf16[128]{0:T(256)(128)(2,1)S(1)} %get-tuple-element.6), kind=kOutput, calls=%fused_computation.28 | convolution fusion | flops 1075838976 | bytes 29360384 | tf_op jit(solution)/shard_map/snj,skj->snk/dot_general | solution.py:92
  280.6 21.6 %fusion.48 = bf16[48,256,128]{2,0,1:T(8,128)(2,1)S(1)} fusion(f32[128,256,128]{2,1,0:T(8,128)} %fusion.21, s32[128]{0:T(128)S(1)} %copy-done.3), kind=kOutput, calls=%fused_computation.57 | convolution fusion | flops 2417498112 | bytes 19923456 | tf_op jit(solution)/shard_map/sc,snj->cnj/dot_general | solution.py:47
  302.2 16.6 %convolution_convert_fusion.6 = bf16[128,256,128]{2,0,1:T(8,128)(2,1)} fusion(s32[128]{0:T(128)S(1)} %copy-done.4, f32[192,256,128]{2,0,1:T(8,128)} %fusion.13), kind=kOutput, calls=%fused_computation.42 | convolution fusion | flops 1671454720 | bytes 33554944 | tf_op jit(solution)/shard_map/sr,rnk->snk/dot_general | solution.py:40
  318.9 19.8 %fusion.25 = f32[128,256,128]{2,1,0:T(8,128)} fusion(bf16[128,256,128]{2,0,1:T(8,128)(2,1)} %convolution_convert_fusion.6, bf16[128,128,128]{2,1,0:T(8,128)(2,1)} %all-gather.5.cloned.1.call-done, bf16[128]{0:T(256)(128)(2,1)S(1)} %get-tuple-element.6), kind=kOutput, calls=%fused_computation.32 | convolution fusion | flops 1075838976 | bytes 29360384 | tf_op jit(solution)/shard_map/snk,skj->snj/dot_general | solution.py:84
  338.7 22.4 %fusion.45 = bf16[48,256,128]{2,0,1:T(8,128)(2,1)} fusion(f32[128,256,128]{2,1,0:T(8,128)} %fusion.25, s32[128]{0:T(128)S(1)} %copy-done.3), kind=kOutput, calls=%fused_computation.56 | convolution fusion | flops 2417498112 | bytes 19923456 | tf_op jit(solution)/shard_map/sc,snj->cnj/dot_general | solution.py:47
  361.1 31.2 %reduce-scatter.5.cloned.1.call-done = f32[4,128,128]{2,1,0:T(8,128)} async-done(((f32[128,128,128]{2,1,0:T(8,128)}), f32[4,128,128]{2,1,0:T(8,128)}) %reduce-scatter.5.cloned.1.call-update) | async-done | bytes 262160 | tf_op jit(solution)/shard_map/reduce_scatter | solution.py:114
  392.3 6.1 %copy_bitcast_fusion = (bf16[256,6144]{1,0:T(8,128)(2,1)}, bf16[256,6144]{1,0:T(8,128)(2,1)}) fusion(bf16[32,8,48,128]{3,2,1,0:T(8,128)(2,1)S(1)} %bitcast.52, bf16[32,8,48,128]{3,2,1,0:T(8,128)(2,1)} %bitcast.53), kind=kLoop, calls=%fused_computation.50 | loop fusion | bytes 12582912 | tf_op jit(solution)/shard_map/reshape | solution.py:31
  398.4 38.9 %all-reduce.3.cloned.1.call-done = (f32[4,128,128]{2,1,0:T(8,128)}, f32[4,128,128]{2,1,0:T(8,128)}) async-done(((f32[4,128,128]{2,1,0:T(8,128)}, f32[4,128,128]{2,1,0:T(8,128)}), (f32[4,128,128]{2,1,0:T(8,128)}, f32[4,128,128]{2,1,0:T(8,128)})) %all-reduce.3.cloned.1.call-update) | async-done | bytes 524304 | tf_op jit(solution)/shard_map/psum | solution.py:120
  437.3 1.9 broadcast_multiply_fusion.2
  (31 shorter events, 0.3 us)
Async XLA Ops:
  7.2 9.3 %copy-start = (s32[32]{0:T(128)S(1)}, s32[32]{0:T(128)}, u32[]{:S(2)}) copy-start(s32[32]{0:T(128)} %param.13) | copy-start | bytes 388
  7.2 6.8 %copy-start.4 = (s32[128]{0:T(128)S(1)}, s32[128]{0:T(128)}, u32[]{:S(2)}) copy-start(s32[128]{0:T(128)} %param.12) | copy-start | bytes 1540
  7.2 8.0 %copy-start.2 = (s32[128]{0:T(128)S(1)}, s32[128]{0:T(128)}, u32[]{:S(2)}) copy-start(s32[128]{0:T(128)} %param.11) | copy-start | bytes 1540
  7.2 51.5 %all-gather.3.cloned.1.call-start = ((), (), s32[]{:S(2)}) async-start(), calls=%async_computation.2 | async-start | bytes 4325376 | tf_op jit(solution)/shard_map/all_gather | solution.py:71
  7.9 100.0 %all-gather.5.cloned.1.call-start = ((), (), s32[]{:S(2)}) async-start(), calls=%async_computation.3 | async-start | bytes 4325376 | tf_op jit(solution)/shard_map/all_gather | solution.py:81
  8.7 352.4 %reduce-scatter.3.cloned.1.call-start = ((), (), s32[]{:S(2)}) async-start(), calls=%async_computation.4 | async-start | bytes 8650752 | tf_op jit(solution)/shard_map/reduce_scatter | solution.py:104
  8.7 4.4 copy-start.7
  26.6 5.6 %copy-start.6 = (bf16[32,8,48,128]{3,2,1,0:T(8,128)(2,1)S(1)}, bf16[32,8,48,128]{3,2,1,0:T(8,128)(2,1)}, u32[]{:S(2)}) copy-start(bf16[32,8,48,128]{3,2,1,0:T(8,128)(2,1)} %copy.23) | copy-start | bytes 9437188
  170.7 4.6 %copy-start.5 = (bf16[192,256,128]{2,0,1:T(8,128)(2,1)}, bf16[192,256,128]{2,0,1:T(8,128)(2,1)S(1)}, u32[]{:S(2)}) copy-start(bf16[192,256,128]{2,0,1:T(8,128)(2,1)S(1)} %fusion.6) | copy-start | bytes 37748740
  204.1 188.2 %reduce-scatter.5.cloned.1.call-start = ((), (), s32[]{:S(2)}) async-start(), calls=%async_computation.5 | async-start | bytes 8650752 | tf_op jit(solution)/shard_map/reduce_scatter | solution.py:114
  250.7 186.5 %all-reduce.3.cloned.1.call-start = ((), (), s32[]{:S(2)}) async-start(), calls=%async_computation.6 | async-start | bytes 1048576 | tf_op jit(solution)/shard_map/psum | solution.py:120
  261.8 18.8 %copy-start.3 = (s32[128]{0:T(128)S(1)}, s32[128]{0:T(128)}, u32[]{:S(2)}) copy-start(s32[128]{0:T(128)} %param.11) | copy-start | bytes 1540
  338.7 100.4 %copy-start.1 = (s32[32]{0:T(128)S(1)}, s32[32]{0:T(128)}, u32[]{:S(2)}) copy-start(s32[32]{0:T(128)} %param.13) | copy-start | bytes 388
Sparse Core Ops, SparseCore 0:
  10.3 48.3 all-gather.2
  61.0 45.3 all-gather.4
  204.2 92.0 reduce-scatter.2
  300.3 91.9 reduce-scatter.4
  394.5 42.6 all-reduce.2
where the time goes:
time: 449 us; the launch traced here: 446 us
  matrix products  316 us (70%)
  waiting for transfers between devices  92.4 us (21%)
  local copies, waits for them, and re-layouts  21 us (5%)
  between operations  14.2 us (3%)
    dot_general x4, matrix products, spread_blocks(): jnp.einsum('sc,snj->cnj', table, contrib, preferred_element_type=jnp.floa...  119 us
    dot_general x8, matrix products, pick_blocks(): jnp.einsum('sr,rnk->snk', table, blocks, preferred_element_type=jnp.float32)  74.6 us
    psum x1, waiting for transfers between devices, on_device(): up_grad, down_grad = lax.psum((up_local, down_local), 'dp')  38.9 us
    reduce_scatter x1, waiting for transfers between devices, on_device(): lax.psum_scatter(jnp.einsum('snk,snj->skj', h_pick, dy_pick, preferred_el...  31.2 us
    dot_general x1, matrix products, on_device(): jnp.einsum('snk,snj->skj', h_pick, dy_pick, preferred_element_type=jnp.fl...  23.8 us
    dot_general x1, matrix products, on_device(): jnp.einsum('snk,snj->skj', x_pick, p_pick, preferred_element_type=jnp.flo...  23.2 us
    all_gather x1, waiting for transfers between devices, on_device(): up_whole = lax.all_gather(up_weight_blocks, 'fsdp', axis=0, tiled=True)  20.9 us
    dot_general x1, matrix products, on_device(): jnp.einsum('snk,skj->snj', h_pick, weights, preferred_element_type=jnp.fl...  19.8 us
  transfers between devices with their start and end apart: 5, of which 3 were waited for; matrix products, arithmetic and copies ran while one was open for 54% of the time, Pallas kernels for 0%

commit v1 on v0

--- a/solution.py
+++ b/solution.py
@@ -68,7 +68,10 @@
     def slot_info():
         return (block_rows, block_cols, live_mask.astype(jnp.bfloat16)[:, None, None])
 
-    up_whole = lax.all_gather(up_weight_blocks, "fsdp", axis=0, tiled=True)
+    size = lax.axis_size("fsdp")
+    parts = jnp.stack([up_weight_blocks for _ in range(size)])
+    parts = lax.all_to_all(parts, "fsdp", split_axis=0, concat_axis=0)
+    up_whole = jnp.concatenate(parts, axis=0)
     row_ids, col_ids, keep_mask = slot_info()
     picked = pick_blocks(x_blocks, row_ids)
     contrib = jnp.einsum(

time: 449 us -> 444 us (0.989)
  waiting for transfers between devices: 92.4 us -> 69.5 us
  local copies, waits for them, and re-layouts: 21 us -> 28.7 us
  starting transfers between devices: 0.2 us -> 7.69 us
    reduce_scatter x1, waiting for transfers between devices: 31.2 us -> 0.01 us  [on_device(): lax.psum_scatter(jnp.einsum('snk,snj->skj', h_pick, dy_pick, preferred_el...]
    all_to_all x0 -> x1, waiting for transfers between devices: none -> 29.6 us  [on_device(): parts = lax.all_to_all(parts, 'fsdp', split_axis=0, concat_axis=0)]
    all_gather x1 -> x0, waiting for transfers between devices: 20.9 us -> none  [on_device(): up_whole = lax.all_gather(up_weight_blocks, 'fsdp', axis=0, tiled=True)]
    all_to_all x0 -> x1, starting transfers between devices: none -> 7.53 us  [on_device(): parts = lax.all_to_all(parts, 'fsdp', split_axis=0, concat_axis=0)]
    unnamed x18 -> x20, local copies, waits for them, and re-layouts: 9.8 us -> 13.3 us
  transfers between devices with their start and end apart: 5 -> 5, of which waited for: 3 -> 2; matrix products, arithmetic and copies ran while one was open for 54% -> 76% of each run, Pallas kernels for 0% -> 0%
where the time goes in v1:
time: 444 us; the launch traced here: 440 us
  matrix products  316 us (71%)
  waiting for transfers between devices  69.5 us (16%)
  local copies, waits for them, and re-layouts  28.7 us (6%)
  between operations  14.2 us (3%)
  starting transfers between devices  7.69 us (2%)
    dot_general x4, matrix products, spread_blocks(): jnp.einsum('sc,snj->cnj', table, contrib, preferred_element_type=jnp.floa...  120 us
    dot_general x8, matrix products, pick_blocks(): jnp.einsum('sr,rnk->snk', table, blocks, preferred_element_type=jnp.float32)  74.8 us
    psum x1, waiting for transfers between devices, on_device(): up_grad, down_grad = lax.psum((up_local, down_local), 'dp')  39.1 us
    all_to_all x1, waiting for transfers between devices, on_device(): parts = lax.all_to_all(parts, 'fsdp', split_axis=0, concat_axis=0)  29.6 us
    dot_general x1, matrix products, on_device(): jnp.einsum('snk,snj->skj', x_pick, p_pick, preferred_element_type=jnp.flo...  23.1 us
    dot_general x1, matrix products, on_device(): jnp.einsum('snk,snj->skj', h_pick, dy_pick, preferred_element_type=jnp.fl...  23 us
    dot_general x1, matrix products, on_device(): jnp.einsum('snj,skj->snk', dy_pick, weights, preferred_element_type=jnp.f...  20.3 us
    dot_general x1, matrix products, on_device(): jnp.einsum('snj,skj->snk', picked, up_whole * keep_mask, preferred_elemen...  19.1 us
  transfers between devices with their start and end apart: 5, of which 2 were waited for; matrix products, arithmetic and copies ran while one was open for 76% of the time, Pallas kernels for 0%

profile of v1, /device:TPU:0, one launch (start us, length us, event | category | flops | bytes accessed | tf_op | source)
XLA Modules:
  0.0 440.1 jit_solution(901417682188429765)
XLA Ops:
  7.2 3.9 stack.2
  11.1 7.5 %all-to-all-start = ((bf16[32,4,128,128]{3,2,1,0:T(8,128)(2,1)}), bf16[32,4,128,128]{3,2,1,0:T(8,128)(2,1)}, u32[]{:S(2)}, u32[]{:S(2)}) async-start(bf16[32,4,128,128]{3,2,1,0:T(8,128)(2,1)} %stack.2), calls=%async_computation | async-start | bytes 8388608 | tf_op jit(solution)/shard_map/all_to_all | solution.py:73
  19.4 2.6 copy.23
  22.1 4.3 copy.25
  26.4 1.2 gather_fusion.2
  28.9 1.2 gather_fusion
  30.1 1.7 gather_fusion.3
  31.9 5.6 %convolution_convert_fusion.7 = bf16[128,256,128]{2,0,1:T(8,128)(2,1)} fusion(bf16[256,48,128]{2,1,0:T(8,128)(2,1)S(1)} %bitcast.52, s32[128]{0:T(128)S(1)} %copy-done.2), kind=kOutput, calls=%fused_computation.43 | convolution fusion | flops 406853632 | bytes 11534848 | tf_op jit(solution)/shard_map/sr,rnk->snk/dot_general | solution.py:40
  37.5 5.6 %convolution_convert_fusion = bf16[128,256,128]{2,0,1:T(8,128)(2,1)} fusion(bf16[256,48,128]{2,1,0:T(8,128)(2,1)S(1)} %bitcast.55, s32[128]{0:T(128)S(1)} %gather_fusion.1), kind=kOutput, calls=%fused_computation.36 | convolution fusion | flops 406853632 | bytes 11534848 | tf_op jit(solution)/shard_map/sr,rnk->snk/dot_general | solution.py:40
  43.1 29.6 %all-to-all-done = bf16[32,4,128,128]{3,2,1,0:T(8,128)(2,1)} async-done(((bf16[32,4,128,128]{3,2,1,0:T(8,128)(2,1)}), bf16[32,4,128,128]{3,2,1,0:T(8,128)(2,1)}, u32[]{:S(2)}, u32[]{:S(2)}) %all-to-all-start) | async-done | bytes 4194336 | tf_op jit(solution)/shard_map/all_to_all | solution.py:73
  72.8 2.5 bitcast_multiply_fusion
  75.3 1.9 copy-done.5
  77.2 17.9 %fusion.27 = f32[128,256,128]{2,1,0:T(8,128)} fusion(bf16[128,128,128]{2,1,0:T(8,128)(2,1)S(1)} %bitcast_multiply_fusion, bf16[128,256,128]{2,0,1:T(8,128)(2,1)} %convolution_convert_fusion.7), kind=kOutput, calls=%fused_computation.34 | convolution fusion | flops 1073741824 | bytes 29360128 | tf_op jit(solution)/shard_map/snk,skj->snj/dot_general | solution.py:77
  95.1 29.9 %fusion.13 = f32[192,256,128]{2,0,1:T(8,128)} fusion(f32[128,256,128]{2,1,0:T(8,128)} %fusion.27, s32[128]{0:T(128)S(1)} %copy-done.3), kind=kOutput, calls=%fused_computation.20 | convolution fusion | flops 9663700992 | bytes 41943552 | tf_op jit(solution)/shard_map/sc,snj->cnj/dot_general | solution.py:47
  125.1 16.9 %convolution_convert_fusion.1 = bf16[128,256,128]{2,0,1:T(8,128)(2,1)} fusion(s32[128]{0:T(128)S(1)} %gather_fusion.2, f32[192,256,128]{2,0,1:T(8,128)} %fusion.13), kind=kOutput, calls=%fused_computation.37 | convolution fusion | flops 1671454720 | bytes 33554944 | tf_op jit(solution)/shard_map/sr,rnk->snk/dot_general | solution.py:40
  142.0 23.0 %broadcast_multiply_fusion = f32[128,128,128]{2,1,0:T(8,128)} fusion(f32[128]{0:T(128)S(1)} %convert_element_type.86, bf16[128,256,128]{2,0,1:T(8,128)(2,1)} %convolution_convert_fusion, bf16[128,256,128]{2,0,1:T(8,128)(2,1)} %convolution_convert_fusion.1), kind=kOutput, calls=%fused_computation.45 | convolution fusion | flops 1075838976 | bytes 25166336 | tf_op jit(solution)/shard_map/snk,snj->skj/dot_general | solution.py:118
  165.0 7.5 %convolution_convert_fusion.5 = bf16[128,256,128]{2,0,1:T(8,128)(2,1)} fusion(bf16[256,48,128]{2,1,0:T(8,128)(2,1)} %bitcast.54, s32[128]{0:T(128)S(1)} %copy-done.2), kind=kOutput, calls=%fused_computation.41 | convolution fusion | flops 406853632 | bytes 11534848 | tf_op jit(solution)/shard_map/sr,rnk->snk/dot_general | solution.py:40
  172.6 5.6 %convolution_convert_fusion.3 = bf16[128,256,128]{2,0,1:T(8,128)(2,1)} fusion(bf16[256,48,128]{2,1,0:T(8,128)(2,1)S(1)} %bitcast.53, s32[128]{0:T(128)S(1)} %gather_fusion.1), kind=kOutput, calls=%fused_computation.39 | convolution fusion | flops 406853632 | bytes 11534848 | tf_op jit(solution)/shard_map/sr,rnk->snk/dot_general | solution.py:40
  178.2 20.3 %fusion.23 = f32[128,256,128]{2,1,0:T(8,128)} fusion(bf16[128,256,128]{2,0,1:T(8,128)(2,1)} %convolution_convert_fusion.5, bf16[128,128,128]{2,1,0:T(8,128)(2,1)} %all-gather.2.cloned.1.call-done, bf16[128]{0:T(256)(128)(2,1)S(1)} %get-tuple-element.6), kind=kOutput, calls=%fused_computation.30 | convolution fusion | flops 1075838976 | bytes 29360384 | tf_op jit(solution)/shard_map/snj,skj->snk/dot_general | solution.py:88
  198.5 44.5 %fusion.6 = bf16[192,256,128]{2,0,1:T(8,128)(2,1)S(1)} fusion(f32[192,256,128]{2,0,1:T(8,128)} %fusion.13, f32[128,256,128]{2,1,0:T(8,128)} %fusion.23, s32[128]{0:T(128)S(1)} %copy-done.3), kind=kOutput, calls=%fused_computation.12 | convolution fusion | flops 9783238656 | bytes 54526464 | tf_op jit(solution)/shard_map/sc,snj->cnj/dot_general | solution.py:47
  243.0 4.5 %copy-done.4 = bf16[192,256,128]{2,0,1:T(8,128)(2,1)} copy-done((bf16[192,256,128]{2,0,1:T(8,128)(2,1)}, bf16[192,256,128]{2,0,1:T(8,128)(2,1)S(1)}, u32[]{:S(2)}) %copy-start.4) | copy-done | bytes 12582936
  247.5 5.7 %convolution_convert_fusion.2 = bf16[128,256,128]{2,0,1:T(8,128)(2,1)} fusion(bf16[192,256,128]{2,0,1:T(8,128)(2,1)S(1)} %fusion.6, s32[128]{0:T(128)S(1)} %gather_fusion.2), kind=kOutput, calls=%fused_computation.38 | convolution fusion | flops 1614831616 | bytes 20972032 | tf_op jit(solution)/shard_map/sr,rnk->snk/dot_general | solution.py:40
  253.2 23.1 %broadcast_multiply_fusion.1 = f32[128,128,128]{2,1,0:T(8,128)} fusion(f32[128]{0:T(128)S(1)} %convert_element_type.86, bf16[128,256,128]{2,0,1:T(8,128)(2,1)} %convolution_convert_fusion.2, bf16[128,256,128]{2,0,1:T(8,128)(2,1)} %convolution_convert_fusion.3), kind=kOutput, calls=%fused_computation.46 | convolution fusion | flops 1075838976 | bytes 25166336 | tf_op jit(solution)/shard_map/snk,snj->skj/dot_general | solution.py:108
  276.5 16.9 %convolution_convert_fusion.6 = bf16[128,256,128]{2,0,1:T(8,128)(2,1)} fusion(s32[128]{0:T(128)S(1)} %copy-done.3, f32[192,256,128]{2,0,1:T(8,128)} %fusion.13), kind=kOutput, calls=%fused_computation.42 | convolution fusion | flops 1671454720 | bytes 33554944 | tf_op jit(solution)/shard_map/sr,rnk->snk/dot_general | solution.py:40
  293.4 10.9 %convolution_convert_fusion.4 = bf16[128,256,128]{2,0,1:T(8,128)(2,1)} fusion(bf16[192,256,128]{2,0,1:T(8,128)(2,1)} %copy-done.4, s32[128]{0:T(128)S(1)} %copy-done.3), kind=kOutput, calls=%fused_computation.40 | convolution fusion | flops 1614831616 | bytes 20972032 | tf_op jit(solution)/shard_map/sr,rnk->snk/dot_general | solution.py:40
  304.2 19.1 %fusion.21 = f32[128,256,128]{2,1,0:T(8,128)} fusion(bf16[128,128,128]{2,1,0:T(8,128)(2,1)} %copy-done.5, bf16[128,256,128]{2,0,1:T(8,128)(2,1)} %convolution_convert_fusion.4), kind=kOutput, calls=%fused_computation.28 | convolution fusion | flops 1073741824 | bytes 29360128 | tf_op jit(solution)/shard_map/snj,skj->snk/dot_general | solution.py:95
  323.3 22.7 %fusion.46 = bf16[48,256,128]{2,0,1:T(8,128)(2,1)} fusion(f32[128,256,128]{2,1,0:T(8,128)} %fusion.21, s32[128]{0:T(128)S(1)} %copy-done.2), kind=kOutput, calls=%fused_computation.56 | convolution fusion | flops 2417498112 | bytes 19923456 | tf_op jit(solution)/shard_map/sc,snj->cnj/dot_general | solution.py:47
  346.0 17.6 %fusion.25 = f32[128,256,128]{2,1,0:T(8,128)} fusion(bf16[128,256,128]{2,0,1:T(8,128)(2,1)} %convolution_convert_fusion.6, bf16[128,128,128]{2,1,0:T(8,128)(2,1)S(1)} %copy-done.7, bf16[128]{0:T(256)(128)(2,1)S(1)} %get-tuple-element.6), kind=kOutput, calls=%fused_computation.32 | convolution fusion | flops 1075838976 | bytes 29360384 | tf_op jit(solution)/shard_map/snk,skj->snj/dot_general | solution.py:87
  363.6 22.5 %fusion.43 = bf16[48,256,128]{2,0,1:T(8,128)(2,1)} fusion(f32[128,256,128]{2,1,0:T(8,128)} %fusion.25, s32[128]{0:T(128)S(1)} %copy-done.2), kind=kOutput, calls=%fused_computation.55 | convolution fusion | flops 2417498112 | bytes 19923456 | tf_op jit(solution)/shard_map/sc,snj->cnj/dot_general | solution.py:47
  386.2 6.1 %copy_bitcast_fusion = (bf16[256,6144]{1,0:T(8,128)(2,1)}, bf16[256,6144]{1,0:T(8,128)(2,1)}) fusion(bf16[32,8,48,128]{3,2,1,0:T(8,128)(2,1)S(1)} %bitcast.56, bf16[32,8,48,128]{3,2,1,0:T(8,128)(2,1)} %bitcast.57), kind=kLoop, calls=%fused_computation.49 | loop fusion | bytes 12582912 | tf_op jit(solution)/shard_map/reshape | solution.py:31
  392.3 39.1 %all-reduce.3.cloned.1.call-done = (f32[4,128,128]{2,1,0:T(8,128)}, f32[4,128,128]{2,1,0:T(8,128)}) async-done(((f32[4,128,128]{2,1,0:T(8,128)}, f32[4,128,128]{2,1,0:T(8,128)}), (f32[4,128,128]{2,1,0:T(8,128)}, f32[4,128,128]{2,1,0:T(8,128)})) %all-reduce.3.cloned.1.call-update) | async-done | bytes 524304 | tf_op jit(solution)/shard_map/psum | solution.py:123
  431.4 1.9 broadcast_multiply_fusion.2
  (34 shorter events, 2.2 us)
Async XLA Ops:
  7.2 21.7 %copy-start = (s32[32]{0:T(128)S(1)}, s32[32]{0:T(128)}, u32[]{:S(2)}) copy-start(s32[32]{0:T(128)} %param.13) | copy-start | bytes 388
  11.1 61.7 %all-to-all-start = ((bf16[32,4,128,128]{3,2,1,0:T(8,128)(2,1)}), bf16[32,4,128,128]{3,2,1,0:T(8,128)(2,1)}, u32[]{:S(2)}, u32[]{:S(2)}) async-start(bf16[32,4,128,128]{3,2,1,0:T(8,128)(2,1)} %stack.2), calls=%async_computation | async-start | bytes 8388608 | tf_op jit(solution)/shard_map/all_to_all | solution.py:73
  18.6 7.7 %copy-start.3 = (s32[128]{0:T(128)S(1)}, s32[128]{0:T(128)}, u32[]{:S(2)}) copy-start(s32[128]{0:T(128)} %param.12) | copy-start | bytes 1540
  18.6 9.0 %copy-start.2 = (s32[128]{0:T(128)S(1)}, s32[128]{0:T(128)}, u32[]{:S(2)}) copy-start(s32[128]{0:T(128)} %param.11) | copy-start | bytes 1540
  18.7 159.5 %all-gather.2.cloned.1.call-start = ((), (), s32[]{:S(2)}) async-start(), calls=%async_computation.3 | async-start | bytes 4325376 | tf_op jit(solution)/shard_map/all_gather | solution.py:84
  19.4 366.8 %reduce-scatter.5.cloned.1.call-start = ((), (), s32[]{:S(2)}) async-start(), calls=%async_computation.5 | async-start | bytes 8650752 | tf_op jit(solution)/shard_map/reduce_scatter | solution.py:117
  31.8 5.7 %copy-start.6 = (bf16[32,8,48,128]{3,2,1,0:T(8,128)(2,1)S(1)}, bf16[32,8,48,128]{3,2,1,0:T(8,128)(2,1)}, u32[]{:S(2)}) copy-start(bf16[32,8,48,128]{3,2,1,0:T(8,128)(2,1)} %copy.25) | copy-start | bytes 9437188
  75.3 1.9 copy-start.5
  165.0 221.2 %reduce-scatter.3.cloned.1.call-start = ((), (), s32[]{:S(2)}) async-start(), calls=%async_computation.4 | async-start | bytes 8650752 | tf_op jit(solution)/shard_map/reduce_scatter | solution.py:107
  243.0 4.5 %copy-start.4 = (bf16[192,256,128]{2,0,1:T(8,128)(2,1)}, bf16[192,256,128]{2,0,1:T(8,128)(2,1)S(1)}, u32[]{:S(2)}) copy-start(bf16[192,256,128]{2,0,1:T(8,128)(2,1)S(1)} %fusion.6) | copy-start | bytes 37748740
  276.4 155.0 %all-reduce.3.cloned.1.call-start = ((), (), s32[]{:S(2)}) async-start(), calls=%async_computation.6 | async-start | bytes 1048576 | tf_op jit(solution)/shard_map/psum | solution.py:123
  323.3 22.7 %copy-start.7 = (bf16[128,128,128]{2,1,0:T(8,128)(2,1)S(1)}, bf16[128,128,128]{2,1,0:T(8,128)(2,1)}, u32[]{:S(2)}) copy-start(bf16[128,128,128]{2,1,0:T(8,128)(2,1)} %all-gather.2.cloned.1.call-done) | copy-start | bytes 12582916
  363.6 22.6 %copy-start.8 = (bf16[48,256,128]{2,0,1:T(8,128)(2,1)S(1)}, bf16[48,256,128]{2,0,1:T(8,128)(2,1)}, u32[]{:S(2)}) copy-start(bf16[48,256,128]{2,0,1:T(8,128)(2,1)} %fusion.46) | copy-start | bytes 9437188
  363.6 69.7 %copy-start.1 = (s32[32]{0:T(128)S(1)}, s32[32]{0:T(128)}, u32[]{:S(2)}) copy-start(s32[32]{0:T(128)} %param.13) | copy-start | bytes 388
Sparse Core Ops, SparseCore 0:
  21.8 72.3 all-gather.1
  165.1 94.1 reduce-scatter.4
  276.5 94.2 reduce-scatter.2
  386.3 45.0 all-reduce.2
